TPU v7x, 32 devices: a whole 2x2x4 slice. The times are simulated.
32 devices in a mesh: lon: 8 (over y, x, core), bal: 4 (over z).
Axes of the slice: x: 2, y: 2, z: 4, core: 2. Of those that a mesh axis runs over, the one named last changes fastest.
Arguments:
- conc: float32 [65536, 128], P(('lon', 'bal')), may hold values from -6 to 6
- neighbours: int32 [512, 8], P(('lon', 'bal')), may hold values from 0 to 511, as said below
- counts: int32 [512], P(('lon', 'bal')), may hold values from 1 to 8
- weights: int32 [512, 8], P(('lon', 'bal')), may hold values from 1 to 15
- zones: int32 [65536], P(('lon', 'bal')), may hold values from 0 to 31
- owners: int32 [65536, 1], P(('lon', 'bal')), may hold values from 0 to 3; in each aligned block of 2048 rows (0 to 2047, 2048 to 4095, ...) at most 1024 rows name the same one
- rate_table: float32 [32, 128], replicated, may hold values from 0.05 to 1
- reaction: bfloat16 [128, 128], replicated, may hold values from -0.5 to 0.5
Outputs:
- conc_out: bfloat16 [65536, 128], P(('lon', 'bal'))
- chem_slots: bfloat16 [131072, 128], P(('lon', 'bal'))
Inputs may be any that keep to these rules, and one draw needn't show every extreme that they name: neighbours[g, k] is a block of the same bal index as g, on the same longitude band or on the band just before or after it, with the bands wrapping around. On every trajectory owner, at most 1024 of its parcels have the same owners value; on some trajectory owners one value is taken exactly 1024 times.
All inputs are finite; a program needn't handle non-finite values.
Results may differ from a plain program's by a relative error of at most 0.0085.
Values may be sent and summed in bfloat16 or wider, within the bound.
No kernel may reach another device: no remote copies, remote signals or barrier semaphores. Data moves between devices by JAX's collectives and lax.ppermute only.
A program may use at most 64 MiB of HBM per device.

v0:
```python
import jax
import jax.numpy as jnp
from jax import lax
from jax.sharding import PartitionSpec as P

BLK = 128
KADJ = 8
ZONES = 32
SUBSTEPS = 12


def extended_2(cells, sides, width):
    for axis, dim in sides:
        count = lax.axis_size(axis)
        head = lax.slice_in_dim(cells, 0, width, axis=dim)
        tail = lax.slice_in_dim(cells, cells.shape[dim] - width, cells.shape[dim], axis=dim)
        cells = jnp.concatenate(
            [
                lax.ppermute(tail, axis, [(i, (i + 1) % count) for i in range(count)]),
                cells,
                lax.ppermute(head, axis, [((i + 1) % count, i) for i in range(count)]),
            ],
            axis=dim,
        )
    return cells


def shifted(value, axis, steps):
    count = lax.axis_size(axis)
    pairs = [(source, (source + steps) % count) for source in range(count)]
    return lax.ppermute(value, axis, pairs)


def chemistry(state, reaction):

    def advance(step_index, current):
        tendency = jnp.dot(
            current.astype(jnp.bfloat16), reaction, preferred_element_type=jnp.float32
        )
        return current + 0.25 * jnp.tanh(tendency)

    return lax.fori_loop(0, SUBSTEPS, advance, state.astype(jnp.float32)).astype(jnp.bfloat16)


def shards(conc, neighbours, counts, weights, zones, owners, rate_table, reaction):
    rows, width = conc.shape
    nblocks = rows // BLK
    lon_count = lax.axis_size("lon")
    bal_count = lax.axis_size("bal")
    device_count = lon_count * bal_count
    self_device = lax.axis_index("lon") * bal_count + lax.axis_index("bal")
    own_blocks = conc.reshape(nblocks, BLK, width)
    extended = extended_2(own_blocks, (("lon", 0),), nblocks)
    used = jnp.arange(KADJ, dtype=jnp.int32)[None, :] < counts[:, None]
    coefs = jnp.where(used, weights.astype(jnp.float32) / 128.0, 0.0)
    local_part = neighbours % nblocks
    apart = (neighbours // nblocks - self_device + device_count) % device_count
    ext_index = (
        jnp.where(apart == 0, nblocks, jnp.where(apart == bal_count, 2 * nblocks, 0)) + local_part
    )
    change = jnp.zeros((nblocks, BLK, width), jnp.float32)
    sent = jnp.zeros((3 * nblocks, BLK, width), jnp.float32)
    for column in range(KADJ):
        flux = coefs[:, column][:, None, None] * (extended[ext_index[:, column]] - own_blocks)
        change = change + flux
        sent = sent.at[ext_index[:, column]].add(flux)
    from_right = shifted(sent[:nblocks].astype(jnp.bfloat16), "lon", -1).astype(jnp.float32)
    from_left = shifted(sent[2 * nblocks :].astype(jnp.bfloat16), "lon", 1).astype(jnp.float32)
    change = change - sent[nblocks : 2 * nblocks] - from_right - from_left
    mixed = (own_blocks + change).reshape(rows, width)
    zone_table = (zones[:, None] == jnp.arange(ZONES, dtype=jnp.int32)[None, :]).astype(jnp.float32)
    rates = jnp.dot(zone_table, rate_table, precision=lax.Precision.HIGHEST)
    moved = (mixed * jnp.exp(-rates)).astype(jnp.bfloat16)
    capacity = 2 * rows // bal_count
    owner = owners[:, 0]
    owner_table = (owner[:, None] == jnp.arange(bal_count, dtype=jnp.int32)[None, :]).astype(
        jnp.int32
    )
    rank = jnp.sum((jnp.cumsum(owner_table, axis=0) - owner_table) * owner_table, axis=1)
    slot = owner * capacity + rank
    conc_out = chemistry(moved, reaction)
    outgoing = jnp.zeros((bal_count * capacity, width), jnp.bfloat16).at[slot].set(conc_out)
    outgoing = outgoing.reshape(bal_count, capacity, width)
    chem_slots = lax.all_to_all(outgoing, "bal", split_axis=0, concat_axis=0, tiled=True).reshape(
        -1, width
    )
    return (conc_out, chem_slots)


def solution(mesh):
    in_specs = (
        P(("lon", "bal"), None),
        P(("lon", "bal"), None),
        P(("lon", "bal")),
        P(("lon", "bal"), None),
        P(("lon", "bal")),
        P(("lon", "bal"), None),
        P(),
        P(),
    )
    out_specs = (P(("lon", "bal"), None), P(("lon", "bal"), None))
    return jax.shard_map(shards, mesh=mesh, in_specs=in_specs, out_specs=out_specs, check_vma=False)
```

profile of v0, /device:TPU:0, one launch (start us, length us, event | category | flops | bytes accessed | tf_op | source)
XLA Modules:
  0.0 134.0 jit_solution(15365341471317218973)
XLA Ops:
  1.2 2.9 %collective-permute-start.1 = (f32[16,128,128]{2,1,0:T(8,128)}, f32[16,128,128]{2,1,0:T(8,128)}, u32[]{:S(2)}, u32[]{:S(2)}) collective-permute-start(f32[16,128,128]{2,1,0:T(8,128)} %bitcast.69), channel_id=1, source_target_pairs={{4,0},{8,4},{12,8},{16,12},{20,16},{24,20},{28,24},{0,28},{5,1},{9... | collective-permute-start | bytes 3145736 | tf_op jit(solution)/shard_map/ppermute | solution.py:21
  7.9 17.5 %collective-permute-done = f32[16,128,128]{2,1,0:T(8,128)S(1)} collective-permute-done((f32[16,128,128]{2,1,0:T(8,128)}, f32[16,128,128]{2,1,0:T(8,128)S(1)}, u32[]{:S(2)}, u32[]{:S(2)}) %collective-permute-start) | collective-permute-done | bytes 1048608 | tf_op jit(solution)/shard_map/ppermute | solution.py:19
  27.0 2.1 %pad_maximum_fusion = f32[48,128,128]{2,1,0:T(8,128)S(1)} fusion(f32[16,128,128]{2,1,0:T(8,128)} %collective-permute-done.1, f32[16,128,128]{2,1,0:T(8,128)} %bitcast.70, f32[16,128,128]{2,1,0:T(8,128)} %copy-done.7), kind=kLoop, calls=%fused_computation.21 | loop fusion | flops 1572864 | bytes 6291456 | tf_op jit(solution)/shard_map/concatenate | solution.py:17
  29.0 1.6 %gather_fusion = f32[16,128,128]{2,1,0:T(8,128)} fusion(f32[48,128,128]{2,1,0:T(8,128)S(1)} %pad_maximum_fusion, s32[1024]{0:T(1024)S(1)} %get-tuple-element.59), kind=kCustom, calls=%fused_computation | custom fusion | bytes 2097216 | tf_op jit(solution)/shard_map/gather | solution.py:64
  30.6 1.6 %gather_fusion.1 = f32[16,128,128]{2,1,0:T(8,128)} fusion(f32[48,128,128]{2,1,0:T(8,128)S(1)} %pad_maximum_fusion, s32[1024]{0:T(1024)S(1)} %get-tuple-element.58), kind=kCustom, calls=%fused_computation.1 | custom fusion | bytes 2097216 | tf_op jit(solution)/shard_map/gather | solution.py:64
  32.3 1.6 %gather_fusion.2 = f32[16,128,128]{2,1,0:T(8,128)} fusion(f32[48,128,128]{2,1,0:T(8,128)S(1)} %pad_maximum_fusion, s32[1024]{0:T(1024)S(1)} %get-tuple-element.57), kind=kCustom, calls=%fused_computation.2 | custom fusion | bytes 2097216 | tf_op jit(solution)/shard_map/gather | solution.py:64
  37.1 1.6 %gather_fusion.5 = f32[16,128,128]{2,1,0:T(8,128)} fusion(f32[48,128,128]{2,1,0:T(8,128)S(1)} %pad_maximum_fusion, s32[1024]{0:T(1024)S(1)} %get-tuple-element.54), kind=kCustom, calls=%fused_computation.5 | custom fusion | bytes 2097216 | tf_op jit(solution)/shard_map/gather | solution.py:64
  38.7 1.6 %gather_fusion.6 = f32[16,128,128]{2,1,0:T(8,128)} fusion(f32[48,128,128]{2,1,0:T(8,128)S(1)} %pad_maximum_fusion, s32[1024]{0:T(1024)S(1)} %get-tuple-element.53), kind=kCustom, calls=%fused_computation.6 | custom fusion | bytes 2097216 | tf_op jit(solution)/shard_map/gather | solution.py:64
  41.9 7.7 %subtract_multiply_fusion = (f32[16,128,128]{2,1,0:T(8,128)}, f32[16,128,128]{2,1,0:T(8,128)}, f32[16,128,128]{2,1,0:T(8,128)}, f32[16,128,128]{2,1,0:T(8,128)},...) fusion(f32[16,128,128]{2,1,0:T(8,128)} %gather_fusion.7, ...), kind=kLoop, calls=%fused_computation.31 | loop fusion | flops 4194304 | bytes 17826304 | tf_op jit(solution)/shard_map/mul | solution.py:64
  50.0 2.6 %scatter_fusion = f32[48,128,128]{2,1,0:T(8,128)S(1)} fusion(f32[48,128,128]{2,1,0:T(8,128)S(1)} %broadcast_in_dim.15, s32[16]{0:T(128)S(1)} %get-tuple-element.51, f32[16,128,128]{2,1,0:T(8,128)} %get-tuple-element.35), kind=kCustom, calls=%fused_computation.8 | custom fusion | flops 262144 | bytes 3145792 | tf_op jit(solution)/shard_map/scatter-add | solution.py:66
  52.6 2.6 %scatter_fusion.1 = f32[48,128,128]{2,1,0:T(8,128)S(1)} fusion(f32[48,128,128]{2,1,0:T(8,128)S(1)} %scatter_fusion, s32[16]{0:T(128)S(1)} %get-tuple-element.50, f32[16,128,128]{2,1,0:T(8,128)} %get-tuple-element.34), kind=kCustom, calls=%fused_computation.9 | custom fusion | flops 262144 | bytes 3145792 | tf_op jit(solution)/shard_map/scatter-add | solution.py:66
  55.2 2.6 %scatter_fusion.2 = f32[48,128,128]{2,1,0:T(8,128)S(1)} fusion(f32[48,128,128]{2,1,0:T(8,128)S(1)} %scatter_fusion.1, s32[16]{0:T(128)S(1)} %get-tuple-element.49, f32[16,128,128]{2,1,0:T(8,128)} %get-tuple-element.33), kind=kCustom, calls=%fused_computation.10 | custom fusion | flops 262144 | bytes 3145792 | tf_op jit(solution)/shard_map/scatter-add | solution.py:66
  57.8 2.6 %scatter_fusion.3 = f32[48,128,128]{2,1,0:T(8,128)S(1)} fusion(f32[48,128,128]{2,1,0:T(8,128)S(1)} %scatter_fusion.2, s32[16]{0:T(128)S(1)} %get-tuple-element.48, f32[16,128,128]{2,1,0:T(8,128)} %get-tuple-element.32), kind=kCustom, calls=%fused_computation.11 | custom fusion | flops 262144 | bytes 3145792 | tf_op jit(solution)/shard_map/scatter-add | solution.py:66
  60.5 2.6 %scatter_fusion.4 = f32[48,128,128]{2,1,0:T(8,128)S(1)} fusion(f32[48,128,128]{2,1,0:T(8,128)S(1)} %scatter_fusion.3, s32[16]{0:T(128)S(1)} %get-tuple-element.47, f32[16,128,128]{2,1,0:T(8,128)} %get-tuple-element.31), kind=kCustom, calls=%fused_computation.12 | custom fusion | flops 262144 | bytes 3145792 | tf_op jit(solution)/shard_map/scatter-add | solution.py:66
  63.1 2.6 %scatter_fusion.5 = f32[48,128,128]{2,1,0:T(8,128)S(1)} fusion(f32[48,128,128]{2,1,0:T(8,128)S(1)} %scatter_fusion.4, s32[16]{0:T(128)S(1)} %get-tuple-element.46, f32[16,128,128]{2,1,0:T(8,128)} %get-tuple-element.30), kind=kCustom, calls=%fused_computation.13 | custom fusion | flops 262144 | bytes 3145792 | tf_op jit(solution)/shard_map/scatter-add | solution.py:66
  65.7 2.6 %scatter_fusion.6 = f32[48,128,128]{2,1,0:T(8,128)S(1)} fusion(f32[48,128,128]{2,1,0:T(8,128)S(1)} %scatter_fusion.5, s32[16]{0:T(128)S(1)} %get-tuple-element.45, f32[16,128,128]{2,1,0:T(8,128)} %get-tuple-element.29), kind=kCustom, calls=%fused_computation.14 | custom fusion | flops 262144 | bytes 3145792 | tf_op jit(solution)/shard_map/scatter-add | solution.py:66
  68.3 2.6 %scatter_fusion.7 = f32[48,128,128]{2,1,0:T(8,128)S(1)} fusion(f32[48,128,128]{2,1,0:T(8,128)S(1)} %scatter_fusion.6, s32[16]{0:T(128)S(1)} %get-tuple-element.44, f32[16,128,128]{2,1,0:T(8,128)} %get-tuple-element.28), kind=kCustom, calls=%fused_computation.15 | custom fusion | flops 262144 | bytes 3145792 | tf_op jit(solution)/shard_map/scatter-add | solution.py:66
  71.3 2.9 %collective-permute-start.2 = (bf16[16,128,128]{2,1,0:T(8,128)(2,1)S(1)}, bf16[16,128,128]{2,1,0:T(8,128)(2,1)S(1)}, u32[]{:S(2)}, u32[]{:S(2)}) collective-permute-start(bf16[16,128,128]{2,1,0:T(8,128)(2,1)S(1)} %get-tuple-element.26), channel_id=1, source_target_pairs={{0,28},{4,0},{8,4},{12,8},{16,12},{20,16},{24,20},{28,24},{1,29},{... | collective-permute-start | bytes 1572872 | tf_op jit(solution)/shard_map/ppermute | solution.py:31
  74.3 12.2 %collective-permute-done.2 = bf16[16,128,128]{2,1,0:T(8,128)(2,1)S(1)} collective-permute-done((bf16[16,128,128]{2,1,0:T(8,128)(2,1)S(1)}, bf16[16,128,128]{2,1,0:T(8,128)(2,1)S(1)}, u32[]{:S(2)}, u32[]{:S(2)}) %collective-permute-start.2) | collective-permute-done | bytes 524320 | tf_op jit(solution)/shard_map/ppermute | solution.py:31
  87.0 3.1 %fusion.6 = f32[16,128,128]{2,1,0:T(8,128)S(1)} fusion(f32[16,128,128]{2,1,0:T(8,128)} %bitcast.72, f32[48,128,128]{2,1,0:T(8,128)S(1)} %scatter_fusion.7, bf16[16,128,128]{2,1,0:T(8,128)(2,1)S(1)} %collective-permute-done.3, bf16[16,128,128]{2,1,0:T(8,128)(2,1)S(1)} %collective-permute-done.2, f32[16,128,128]{2,1,0:T(8,128)S(1)} %copy-done.1, ...), kind=kLoop, calls=%fused_computation.27 | loop fusion | flops 3407872 | bytes 12582912 | tf_op jit(solution)/shard_map/add | solution.py:70
  91.1 4.7 %while.10 = (s32[]{:T(128)}, f32[2048,128]{1,0:T(8,128)S(1)}, bf16[128,128]{1,0:T(8,128)(2,1)S(1)}, s32[]{:T(128)}) while((s32[]{:T(128)}, f32[2048,128]{1,0:T(8,128)S(1)}, bf16[128,128]{1,0:T(8,128)(2,1)S(1)}, s32[]{:T(128)}) %tuple.53), condition=%wide.region_9.10_spmd, body=%wide.region_8.9_spmd.sunk | while | flops 67895296 | bytes 4227125 | solution.py:42
  95.8 6.8 %scatter_custom_fusion.8 = bf16[4096,128]{1,0:T(8,128)(2,1)} fusion(s32[2048]{0:T(1024)S(1)} %bitcast.77, bf16[]{:T(256)} %constant.76.clone.1, f32[2048,128]{1,0:T(8,128)S(1)} %get-tuple-element.19), kind=kCustom, calls=%fused_computation.40 | custom fusion | flops 262144 | bytes 2097154 | tf_op jit(solution)/shard_map/scatter | solution.py:82
  102.6 5.6 %all-to-all-start = ((bf16[4,1024,128]{2,1,0:T(8,128)(2,1)}), bf16[4,1024,128]{2,1,0:T(8,128)(2,1)S(1)}, u32[]{:S(2)}, u32[]{:S(2)}) async-start(bf16[4,1024,128]{2,1,0:T(8,128)(2,1)} %bitcast.23), calls=%async_computation | async-start | bytes 2097152 | tf_op jit(solution)/shard_map/all_to_all | solution.py:84
  109.1 24.0 %all-to-all-done = bf16[4,1024,128]{2,1,0:T(8,128)(2,1)S(1)} async-done(((bf16[4,1024,128]{2,1,0:T(8,128)(2,1)}), bf16[4,1024,128]{2,1,0:T(8,128)(2,1)S(1)}, u32[]{:S(2)}, u32[]{:S(2)}) %all-to-all-start) | async-done | bytes 1048608 | tf_op jit(solution)/shard_map/all_to_all | solution.py:84
  (74 shorter events, 19.0 us)
Async XLA Ops:
  0.6 89.4 %copy-start = (f32[32,128]{1,0:T(8,128)S(1)}, f32[32,128]{1,0:T(8,128)}, u32[]{:S(2)}) copy-start(f32[32,128]{1,0:T(8,128)} %param.16) | copy-start | bytes 49156
  0.6 24.8 %collective-permute-start = (f32[16,128,128]{2,1,0:T(8,128)}, f32[16,128,128]{2,1,0:T(8,128)S(1)}, u32[]{:S(2)}, u32[]{:S(2)}) collective-permute-start(f32[16,128,128]{2,1,0:T(8,128)} %bitcast.68), channel_id=1, source_target_pairs={{0,4},{4,8},{8,12},{12,16},{16,20},{20,24},{24,28},{28,0},{1,5},{5... | collective-permute-start | bytes 3145736 | tf_op jit(solution)/shard_map/ppermute | solution.py:19
  1.2 25.8 %collective-permute-start.1 = (f32[16,128,128]{2,1,0:T(8,128)}, f32[16,128,128]{2,1,0:T(8,128)}, u32[]{:S(2)}, u32[]{:S(2)}) collective-permute-start(f32[16,128,128]{2,1,0:T(8,128)} %bitcast.69), channel_id=1, source_target_pairs={{4,0},{8,4},{12,8},{16,12},{20,16},{24,20},{28,24},{0,28},{5,1},{9... | collective-permute-start | bytes 3145736 | tf_op jit(solution)/shard_map/ppermute | solution.py:21
  25.4 1.0 copy-start.7
  70.9 3.3 %copy-start.9 = (s32[2048,1]{0,1:T(1,128)S(1)}, s32[2048,1]{0,1:T(1,128)}, u32[]{:S(2)}) copy-start(s32[2048,1]{0,1:T(1,128)} %param.15) | copy-start | bytes 24580
  70.9 16.0 %copy-start.1 = (f32[16,128,128]{2,1,0:T(8,128)S(1)}, f32[16,128,128]{2,1,0:T(8,128)}, u32[]{:S(2)}) copy-start(f32[16,128,128]{2,1,0:T(8,128)} %get-tuple-element.28) | copy-start | bytes 3145732
  70.9 16.0 %copy-start.2 = (f32[16,128,128]{2,1,0:T(8,128)S(1)}, f32[16,128,128]{2,1,0:T(8,128)}, u32[]{:S(2)}) copy-start(f32[16,128,128]{2,1,0:T(8,128)} %get-tuple-element.29) | copy-start | bytes 3145732
  71.0 16.0 %copy-start.3 = (f32[16,128,128]{2,1,0:T(8,128)S(1)}, f32[16,128,128]{2,1,0:T(8,128)}, u32[]{:S(2)}) copy-start(f32[16,128,128]{2,1,0:T(8,128)} %get-tuple-element.30) | copy-start | bytes 3145732
  71.0 16.0 %copy-start.4 = (f32[16,128,128]{2,1,0:T(8,128)S(1)}, f32[16,128,128]{2,1,0:T(8,128)}, u32[]{:S(2)}) copy-start(f32[16,128,128]{2,1,0:T(8,128)} %get-tuple-element.31) | copy-start | bytes 3145732
  71.0 16.0 %copy-start.5 = (f32[16,128,128]{2,1,0:T(8,128)S(1)}, f32[16,128,128]{2,1,0:T(8,128)}, u32[]{:S(2)}) copy-start(f32[16,128,128]{2,1,0:T(8,128)} %get-tuple-element.32) | copy-start | bytes 3145732
  71.0 16.0 %copy-start.6 = (f32[16,128,128]{2,1,0:T(8,128)S(1)}, f32[16,128,128]{2,1,0:T(8,128)}, u32[]{:S(2)}) copy-start(f32[16,128,128]{2,1,0:T(8,128)} %get-tuple-element.33) | copy-start | bytes 3145732
  71.3 15.2 %collective-permute-start.2 = (bf16[16,128,128]{2,1,0:T(8,128)(2,1)S(1)}, bf16[16,128,128]{2,1,0:T(8,128)(2,1)S(1)}, u32[]{:S(2)}, u32[]{:S(2)}) collective-permute-start(bf16[16,128,128]{2,1,0:T(8,128)(2,1)S(1)} %get-tuple-element.26), channel_id=1, source_target_pairs={{0,28},{4,0},{8,4},{12,8},{16,12},{20,16},{24,20},{28,24},{1,29},{... | collective-permute-start | bytes 1572872 | tf_op jit(solution)/shard_map/ppermute | solution.py:31
  74.2 12.7 %collective-permute-start.3 = (bf16[16,128,128]{2,1,0:T(8,128)(2,1)S(1)}, bf16[16,128,128]{2,1,0:T(8,128)(2,1)S(1)}, u32[]{:S(2)}, u32[]{:S(2)}) collective-permute-start(bf16[16,128,128]{2,1,0:T(8,128)(2,1)S(1)} %get-tuple-element.27), channel_id=1, source_target_pairs={{0,4},{4,8},{8,12},{12,16},{16,20},{20,24},{24,28},{28,0},{1,5},{5... | collective-permute-start | bytes 1572872 | tf_op jit(solution)/shard_map/ppermute | solution.py:31
  74.3 15.8 %copy-start.10 = (s32[2048]{0:T(1024)S(1)}, s32[2048]{0:T(1024)}, u32[]{:S(2)}) copy-start(s32[2048]{0:T(1024)} %param.14) | copy-start | bytes 24580
  74.3 16.8 %copy-start.8 = (bf16[128,128]{1,0:T(8,128)(2,1)S(1)}, bf16[128,128]{1,0:T(8,128)(2,1)}, u32[]{:S(2)}) copy-start(bf16[128,128]{1,0:T(8,128)(2,1)} %param.17) | copy-start | bytes 98308
  102.6 30.5 %all-to-all-start = ((bf16[4,1024,128]{2,1,0:T(8,128)(2,1)}), bf16[4,1024,128]{2,1,0:T(8,128)(2,1)S(1)}, u32[]{:S(2)}, u32[]{:S(2)}) async-start(bf16[4,1024,128]{2,1,0:T(8,128)(2,1)} %bitcast.23), calls=%async_computation | async-start | bytes 2097152 | tf_op jit(solution)/shard_map/all_to_all | solution.py:84
where the time goes:
time: 135 us; the launch traced here: 134 us
  waiting for transfers between devices  54.7 us (41%)
  other arithmetic  45.2 us (33%)
  local copies, waits for them, and re-layouts  16.3 us (12%)
  starting transfers between devices  12 us (9%)
  matrix products  4.52 us (3%)
    all_to_all x1, waiting for transfers between devices, shards(): lax.all_to_all(outgoing, 'bal', split_axis=0, concat_axis=0, tiled=True)  24 us
    scatter-add x8, other arithmetic, shards(): sent = sent.at[ext_index[:, column]].add(flux)  20.9 us
    ppermute x1, waiting for transfers between devices, extended_2(): lax.ppermute(tail, axis, [(i, (i + 1) % count) for i in range(count)])  17.5 us
    gather x8, local copies, waits for them, and re-layouts, shards(): extended[ext_index[:, column]] - own_blocks  12.9 us
    ppermute x2, waiting for transfers between devices, shifted(): return lax.ppermute(value, axis, pairs)  12.6 us
    mul x1, other arithmetic, shards(): coefs[:, column][:, None, None]  7.75 us
    scatter x1, other arithmetic, shards(): jnp.zeros((bal_count * capacity, width), jnp.bfloat16).at[slot]  6.78 us
    all_to_all x1, starting transfers between devices, shards(): lax.all_to_all(outgoing, 'bal', split_axis=0, concat_axis=0, tiled=True)  5.63 us
  transfers between devices with their start and end apart: 5, of which 5 were waited for; matrix products, arithmetic and copies ran while one was open for 3% of the time, Pallas kernels for 0%

commit v1 on v0

--- a/solution.py
+++ b/solution.py
@@ -7,6 +7,29 @@
 KADJ = 8
 ZONES = 32
 SUBSTEPS = 12
+
+
+def cut_along(x, dim, devices):
+    dims = x.shape
+    blocks = x.reshape(*dims[:dim], devices, dims[dim] // devices, *dims[dim + 1 :])
+    return jnp.moveaxis(blocks, dim, 0)
+
+
+def laid_out(pieces, dim):
+    pieces = jnp.moveaxis(pieces, 0, dim)
+    lengths = pieces.shape
+    return pieces.reshape(*lengths[:dim], lengths[dim] * lengths[dim + 1], *lengths[dim + 2 :])
+
+
+def exchange_directly(value, axis, split_dim, concat_dim):
+    size, mine = (lax.axis_size(axis), lax.axis_index(axis))
+    blocks = cut_along(value, split_dim, size)
+    outs = [blocks[mine]]
+    for hop in range(1, size):
+        sent = blocks[(mine + hop) % size]
+        outs.append(lax.ppermute(sent, axis, [(i, (i + hop) % size) for i in range(size)]))
+    blocks = jnp.stack(outs)[(mine - jnp.arange(size)) % size]
+    return laid_out(blocks, concat_dim)
 
 
 def extended_2(cells, sides, width):
@@ -81,9 +104,7 @@
     conc_out = chemistry(moved, reaction)
     outgoing = jnp.zeros((bal_count * capacity, width), jnp.bfloat16).at[slot].set(conc_out)
     outgoing = outgoing.reshape(bal_count, capacity, width)
-    chem_slots = lax.all_to_all(outgoing, "bal", split_axis=0, concat_axis=0, tiled=True).reshape(
-        -1, width
-    )
+    chem_slots = exchange_directly(outgoing, "bal", 0, 0).reshape(-1, width)
     return (conc_out, chem_slots)
 
 

time: 135 us -> 130 us (0.963)
  the two profiles are of different devices: /device:TPU:0 before, /device:TPU:11 now
where the time goes in v1:
time: 130 us; the launch traced here: 129 us
  waiting for transfers between devices  53.1 us (41%)
  other arithmetic  44.6 us (34%)
  local copies, waits for them, and re-layouts  17.1 us (13%)
  starting transfers between devices  8.35 us (6%)
  matrix products  4.51 us (3%)
    ppermute x3, waiting for transfers between devices, exchange_directly(): lax.ppermute(sent, axis, [(i, (i + hop) % size) for i in range(size)])  21.3 us
    scatter-add x8, other arithmetic, shards(): sent = sent.at[ext_index[:, column]].add(flux)  20.9 us
    ppermute x1, waiting for transfers between devices, extended_2(): lax.ppermute(tail, axis, [(i, (i + 1) % count) for i in range(count)])  18.6 us
    gather x8, local copies, waits for them, and re-layouts, shards(): extended[ext_index[:, column]] - own_blocks  12.9 us
    ppermute x2, waiting for transfers between devices, shifted(): return lax.ppermute(value, axis, pairs)  11.6 us
    mul x1, other arithmetic, shards(): coefs[:, column][:, None, None]  7.75 us
    scatter x1, other arithmetic, shards(): jnp.zeros((bal_count * capacity, width), jnp.bfloat16).at[slot]  6.05 us
    ppermute x3, starting transfers between devices, exchange_directly(): lax.ppermute(sent, axis, [(i, (i + hop) % size) for i in range(size)])  3.83 us
  transfers between devices with their start and end apart: 7, of which 6 were waited for; matrix products, arithmetic and copies ran while one was open for 4% of the time, Pallas kernels for 0%

profile of v1, /device:TPU:11, one launch (start us, length us, event | category | flops | bytes accessed | tf_op | source)
XLA Modules:
  0.0 129.0 jit_solution(17770512866854425182)
XLA Ops:
  0.6 1.8 %collective-permute-start = (f32[16,128,128]{2,1,0:T(8,128)}, f32[16,128,128]{2,1,0:T(8,128)S(1)}, u32[]{:S(2)}, u32[]{:S(2)}) collective-permute-start(f32[16,128,128]{2,1,0:T(8,128)} %bitcast.81), channel_id=1, source_target_pairs={{0,4},{4,8},{8,12},{12,16},{16,20},{20,24},{24,28},{28,0},{1,5},{5... | collective-permute-start | bytes 3145736 | tf_op jit(solution)/shard_map/ppermute | solution.py:42
  6.3 18.6 %collective-permute-done = f32[16,128,128]{2,1,0:T(8,128)S(1)} collective-permute-done((f32[16,128,128]{2,1,0:T(8,128)}, f32[16,128,128]{2,1,0:T(8,128)S(1)}, u32[]{:S(2)}, u32[]{:S(2)}) %collective-permute-start) | collective-permute-done | bytes 1048608 | tf_op jit(solution)/shard_map/ppermute | solution.py:42
  27.4 2.1 %pad_maximum_fusion = f32[48,128,128]{2,1,0:T(8,128)S(1)} fusion(f32[16,128,128]{2,1,0:T(8,128)} %collective-permute-done.1, f32[16,128,128]{2,1,0:T(8,128)} %bitcast.83, f32[16,128,128]{2,1,0:T(8,128)} %copy-done.7), kind=kLoop, calls=%fused_computation.22 | loop fusion | flops 1572864 | bytes 6291456 | tf_op jit(solution)/shard_map/concatenate | solution.py:40
  31.1 1.6 %gather_fusion.1 = f32[16,128,128]{2,1,0:T(8,128)} fusion(f32[48,128,128]{2,1,0:T(8,128)S(1)} %pad_maximum_fusion, s32[1024]{0:T(1024)S(1)} %get-tuple-element.62), kind=kCustom, calls=%fused_computation.1 | custom fusion | bytes 2097216 | tf_op jit(solution)/shard_map/gather | solution.py:87
  37.5 1.6 %gather_fusion.5 = f32[16,128,128]{2,1,0:T(8,128)} fusion(f32[48,128,128]{2,1,0:T(8,128)S(1)} %pad_maximum_fusion, s32[1024]{0:T(1024)S(1)} %get-tuple-element.58), kind=kCustom, calls=%fused_computation.5 | custom fusion | bytes 2097216 | tf_op jit(solution)/shard_map/gather | solution.py:87
  39.1 1.6 %gather_fusion.6 = f32[16,128,128]{2,1,0:T(8,128)} fusion(f32[48,128,128]{2,1,0:T(8,128)S(1)} %pad_maximum_fusion, s32[1024]{0:T(1024)S(1)} %get-tuple-element.57), kind=kCustom, calls=%fused_computation.6 | custom fusion | bytes 2097216 | tf_op jit(solution)/shard_map/gather | solution.py:87
  42.3 7.7 %subtract_multiply_fusion = (f32[16,128,128]{2,1,0:T(8,128)}, f32[16,128,128]{2,1,0:T(8,128)}, f32[16,128,128]{2,1,0:T(8,128)}, f32[16,128,128]{2,1,0:T(8,128)},...) fusion(f32[16,128,128]{2,1,0:T(8,128)} %gather_fusion.7, ...), kind=kLoop, calls=%fused_computation.33 | loop fusion | flops 4194304 | bytes 17826304 | tf_op jit(solution)/shard_map/mul | solution.py:87
  50.5 2.6 %scatter_fusion = f32[48,128,128]{2,1,0:T(8,128)S(1)} fusion(f32[48,128,128]{2,1,0:T(8,128)S(1)} %broadcast_in_dim.15, s32[16]{0:T(128)S(1)} %get-tuple-element.55, f32[16,128,128]{2,1,0:T(8,128)} %get-tuple-element.39), kind=kCustom, calls=%fused_computation.9 | custom fusion | flops 262144 | bytes 3145792 | tf_op jit(solution)/shard_map/scatter-add | solution.py:89
  53.1 2.6 %scatter_fusion.1 = f32[48,128,128]{2,1,0:T(8,128)S(1)} fusion(f32[48,128,128]{2,1,0:T(8,128)S(1)} %scatter_fusion, s32[16]{0:T(128)S(1)} %get-tuple-element.54, f32[16,128,128]{2,1,0:T(8,128)} %get-tuple-element.38), kind=kCustom, calls=%fused_computation.10 | custom fusion | flops 262144 | bytes 3145792 | tf_op jit(solution)/shard_map/scatter-add | solution.py:89
  55.7 2.6 %scatter_fusion.2 = f32[48,128,128]{2,1,0:T(8,128)S(1)} fusion(f32[48,128,128]{2,1,0:T(8,128)S(1)} %scatter_fusion.1, s32[16]{0:T(128)S(1)} %get-tuple-element.53, f32[16,128,128]{2,1,0:T(8,128)} %get-tuple-element.37), kind=kCustom, calls=%fused_computation.11 | custom fusion | flops 262144 | bytes 3145792 | tf_op jit(solution)/shard_map/scatter-add | solution.py:89
  58.3 2.6 %scatter_fusion.3 = f32[48,128,128]{2,1,0:T(8,128)S(1)} fusion(f32[48,128,128]{2,1,0:T(8,128)S(1)} %scatter_fusion.2, s32[16]{0:T(128)S(1)} %get-tuple-element.52, f32[16,128,128]{2,1,0:T(8,128)} %get-tuple-element.36), kind=kCustom, calls=%fused_computation.12 | custom fusion | flops 262144 | bytes 3145792 | tf_op jit(solution)/shard_map/scatter-add | solution.py:89
  60.9 2.6 %scatter_fusion.4 = f32[48,128,128]{2,1,0:T(8,128)S(1)} fusion(f32[48,128,128]{2,1,0:T(8,128)S(1)} %scatter_fusion.3, s32[16]{0:T(128)S(1)} %get-tuple-element.51, f32[16,128,128]{2,1,0:T(8,128)} %get-tuple-element.35), kind=kCustom, calls=%fused_computation.13 | custom fusion | flops 262144 | bytes 3145792 | tf_op jit(solution)/shard_map/scatter-add | solution.py:89
  63.5 2.6 %scatter_fusion.5 = f32[48,128,128]{2,1,0:T(8,128)S(1)} fusion(f32[48,128,128]{2,1,0:T(8,128)S(1)} %scatter_fusion.4, s32[16]{0:T(128)S(1)} %get-tuple-element.50, f32[16,128,128]{2,1,0:T(8,128)} %get-tuple-element.34), kind=kCustom, calls=%fused_computation.14 | custom fusion | flops 262144 | bytes 3145792 | tf_op jit(solution)/shard_map/scatter-add | solution.py:89
  66.1 2.6 %scatter_fusion.6 = f32[48,128,128]{2,1,0:T(8,128)S(1)} fusion(f32[48,128,128]{2,1,0:T(8,128)S(1)} %scatter_fusion.5, s32[16]{0:T(128)S(1)} %get-tuple-element.49, f32[16,128,128]{2,1,0:T(8,128)} %get-tuple-element.33), kind=kCustom, calls=%fused_computation.15 | custom fusion | flops 262144 | bytes 3145792 | tf_op jit(solution)/shard_map/scatter-add | solution.py:89
  68.8 2.6 %scatter_fusion.7 = f32[48,128,128]{2,1,0:T(8,128)S(1)} fusion(f32[48,128,128]{2,1,0:T(8,128)S(1)} %scatter_fusion.6, s32[16]{0:T(128)S(1)} %get-tuple-element.48, f32[16,128,128]{2,1,0:T(8,128)} %get-tuple-element.32), kind=kCustom, calls=%fused_computation.16 | custom fusion | flops 262144 | bytes 3145792 | tf_op jit(solution)/shard_map/scatter-add | solution.py:89
  71.9 2.6 %collective-permute-start.3 = (bf16[16,128,128]{2,1,0:T(8,128)(2,1)S(1)}, bf16[16,128,128]{2,1,0:T(8,128)(2,1)S(1)}, u32[]{:S(2)}, u32[]{:S(2)}) collective-permute-start(bf16[16,128,128]{2,1,0:T(8,128)(2,1)S(1)} %get-tuple-element.27), channel_id=1, source_target_pairs={{0,4},{4,8},{8,12},{12,16},{16,20},{20,24},{24,28},{28,0},{1,5},{5... | collective-permute-start | bytes 1572872 | tf_op jit(solution)/shard_map/ppermute | solution.py:54
  74.6 11.6 %collective-permute-done.2 = bf16[16,128,128]{2,1,0:T(8,128)(2,1)S(1)} collective-permute-done((bf16[16,128,128]{2,1,0:T(8,128)(2,1)S(1)}, bf16[16,128,128]{2,1,0:T(8,128)(2,1)S(1)}, u32[]{:S(2)}, u32[]{:S(2)}) %collective-permute-start.2) | collective-permute-done | bytes 524320 | tf_op jit(solution)/shard_map/ppermute | solution.py:54
  86.2 3.1 %fusion.6 = f32[16,128,128]{2,1,0:T(8,128)S(1)} fusion(f32[16,128,128]{2,1,0:T(8,128)} %bitcast.85, f32[48,128,128]{2,1,0:T(8,128)S(1)} %scatter_fusion.7, bf16[16,128,128]{2,1,0:T(8,128)(2,1)S(1)} %collective-permute-done.3, bf16[16,128,128]{2,1,0:T(8,128)(2,1)S(1)} %collective-permute-done.2, f32[16,128,128]{2,1,0:T(8,128)S(1)} %copy-done.1, ...), kind=kLoop, calls=%fused_computation.28 | loop fusion | flops 3407872 | bytes 12582912 | tf_op jit(solution)/shard_map/add | solution.py:93
  90.4 4.7 %while.10 = (s32[]{:T(128)}, f32[2048,128]{1,0:T(8,128)S(1)}, bf16[128,128]{1,0:T(8,128)(2,1)S(1)}, s32[]{:T(128)}) while((s32[]{:T(128)}, f32[2048,128]{1,0:T(8,128)S(1)}, bf16[128,128]{1,0:T(8,128)(2,1)S(1)}, s32[]{:T(128)}) %tuple.54), condition=%wide.region_9.10_spmd, body=%wide.region_8.9_spmd.sunk | while | flops 67895296 | bytes 4227125 | solution.py:65
  95.0 6.0 %scatter_custom_fusion.8 = bf16[4096,128]{1,0:T(8,128)(2,1)S(1)} fusion(s32[2048]{0:T(1024)S(1)} %bitcast.94, bf16[]{:T(256)} %constant.106.clone.1, f32[2048,128]{1,0:T(8,128)S(1)} %get-tuple-element.19), kind=kCustom, calls=%fused_computation.42 | custom fusion | flops 262144 | bytes 2097154 | tf_op jit(solution)/shard_map/scatter | solution.py:105
  105.9 2.7 %collective-permute-done.4 = bf16[1,1024,128]{2,1,0:T(8,128)(2,1)S(1)} collective-permute-done((bf16[1,1024,128]{2,1,0:T(8,128)(2,1)S(1)}, bf16[1,1024,128]{2,1,0:T(8,128)(2,1)S(1)}, u32[]{:S(2)}, u32[]{:S(2)}) %collective-permute-start.4) | collective-permute-done | bytes 262176 | tf_op jit(solution)/shard_map/ppermute | solution.py:30
  108.6 15.9 %collective-permute-done.5 = bf16[1,1024,128]{2,1,0:T(8,128)(2,1)S(1)} collective-permute-done((bf16[1,1024,128]{2,1,0:T(8,128)(2,1)S(1)}, bf16[1,1024,128]{2,1,0:T(8,128)(2,1)S(1)}, u32[]{:S(2)}, u32[]{:S(2)}) %collective-permute-start.5) | collective-permute-done | bytes 262176 | tf_op jit(solution)/shard_map/ppermute | solution.py:30
  124.5 2.7 %collective-permute-done.6 = bf16[1,1024,128]{2,1,0:T(8,128)(2,1)S(1)} collective-permute-done((bf16[1,1024,128]{2,1,0:T(8,128)(2,1)S(1)}, bf16[1,1024,128]{2,1,0:T(8,128)(2,1)S(1)}, u32[]{:S(2)}, u32[]{:S(2)}) %collective-permute-start.6) | collective-permute-done | bytes 262176 | tf_op jit(solution)/shard_map/ppermute | solution.py:30
  127.4 1.7 %gather_fusion.8 = bf16[4,1024,128]{2,1,0:T(8,128)(2,1)} fusion(bf16[4,1024,128]{2,1,0:T(8,128)(2,1)S(1)} %maximum_bitcast_fusion, s32[1024]{0:T(1024)S(1)} %pad_clamp_fusion), kind=kCustom, calls=%fused_computation.8 | custom fusion | bytes 2097168 | tf_op jit(solution)/shard_map/gather | solution.py:31
  (82 shorter events, 25.3 us)
Async XLA Ops:
  0.6 88.7 %copy-start = (f32[32,128]{1,0:T(8,128)S(1)}, f32[32,128]{1,0:T(8,128)}, u32[]{:S(2)}) copy-start(f32[32,128]{1,0:T(8,128)} %param.16) | copy-start | bytes 49156
  0.6 24.3 %collective-permute-start = (f32[16,128,128]{2,1,0:T(8,128)}, f32[16,128,128]{2,1,0:T(8,128)S(1)}, u32[]{:S(2)}, u32[]{:S(2)}) collective-permute-start(f32[16,128,128]{2,1,0:T(8,128)} %bitcast.81), channel_id=1, source_target_pairs={{0,4},{4,8},{8,12},{12,16},{16,20},{20,24},{24,28},{28,0},{1,5},{5... | collective-permute-start | bytes 3145736 | tf_op jit(solution)/shard_map/ppermute | solution.py:42
  2.5 24.9 %collective-permute-start.1 = (f32[16,128,128]{2,1,0:T(8,128)}, f32[16,128,128]{2,1,0:T(8,128)}, u32[]{:S(2)}, u32[]{:S(2)}) collective-permute-start(f32[16,128,128]{2,1,0:T(8,128)} %bitcast.82), channel_id=1, source_target_pairs={{4,0},{8,4},{12,8},{16,12},{20,16},{24,20},{28,24},{0,28},{5,1},{9... | collective-permute-start | bytes 3145736 | tf_op jit(solution)/shard_map/ppermute | solution.py:44
  24.9 1.0 copy-start.7
  71.4 3.1 %copy-start.9 = (s32[2048,1]{0,1:T(1,128)S(1)}, s32[2048,1]{0,1:T(1,128)}, u32[]{:S(2)}) copy-start(s32[2048,1]{0,1:T(1,128)} %param.15) | copy-start | bytes 24580
  71.4 14.8 %copy-start.1 = (f32[16,128,128]{2,1,0:T(8,128)S(1)}, f32[16,128,128]{2,1,0:T(8,128)}, u32[]{:S(2)}) copy-start(f32[16,128,128]{2,1,0:T(8,128)} %get-tuple-element.32) | copy-start | bytes 3145732
  71.4 14.8 %copy-start.2 = (f32[16,128,128]{2,1,0:T(8,128)S(1)}, f32[16,128,128]{2,1,0:T(8,128)}, u32[]{:S(2)}) copy-start(f32[16,128,128]{2,1,0:T(8,128)} %get-tuple-element.33) | copy-start | bytes 3145732
  71.4 14.8 %copy-start.3 = (f32[16,128,128]{2,1,0:T(8,128)S(1)}, f32[16,128,128]{2,1,0:T(8,128)}, u32[]{:S(2)}) copy-start(f32[16,128,128]{2,1,0:T(8,128)} %get-tuple-element.34) | copy-start | bytes 3145732
  71.4 14.8 %copy-start.4 = (f32[16,128,128]{2,1,0:T(8,128)S(1)}, f32[16,128,128]{2,1,0:T(8,128)}, u32[]{:S(2)}) copy-start(f32[16,128,128]{2,1,0:T(8,128)} %get-tuple-element.35) | copy-start | bytes 3145732
  71.4 14.8 %copy-start.5 = (f32[16,128,128]{2,1,0:T(8,128)S(1)}, f32[16,128,128]{2,1,0:T(8,128)}, u32[]{:S(2)}) copy-start(f32[16,128,128]{2,1,0:T(8,128)} %get-tuple-element.36) | copy-start | bytes 3145732
  71.4 14.8 %copy-start.6 = (f32[16,128,128]{2,1,0:T(8,128)S(1)}, f32[16,128,128]{2,1,0:T(8,128)}, u32[]{:S(2)}) copy-start(f32[16,128,128]{2,1,0:T(8,128)} %get-tuple-element.37) | copy-start | bytes 3145732
  71.8 14.4 %collective-permute-start.2 = (bf16[16,128,128]{2,1,0:T(8,128)(2,1)S(1)}, bf16[16,128,128]{2,1,0:T(8,128)(2,1)S(1)}, u32[]{:S(2)}, u32[]{:S(2)}) collective-permute-start(bf16[16,128,128]{2,1,0:T(8,128)(2,1)S(1)} %get-tuple-element.26), channel_id=1, source_target_pairs={{0,28},{4,0},{8,4},{12,8},{16,12},{20,16},{24,20},{28,24},{1,29},{... | collective-permute-start | bytes 1572872 | tf_op jit(solution)/shard_map/ppermute | solution.py:54
  71.9 14.3 %collective-permute-start.3 = (bf16[16,128,128]{2,1,0:T(8,128)(2,1)S(1)}, bf16[16,128,128]{2,1,0:T(8,128)(2,1)S(1)}, u32[]{:S(2)}, u32[]{:S(2)}) collective-permute-start(bf16[16,128,128]{2,1,0:T(8,128)(2,1)S(1)} %get-tuple-element.27), channel_id=1, source_target_pairs={{0,4},{4,8},{8,12},{12,16},{16,20},{20,24},{24,28},{28,0},{1,5},{5... | collective-permute-start | bytes 1572872 | tf_op jit(solution)/shard_map/ppermute | solution.py:54
  74.6 14.7 %copy-start.10 = (s32[2048]{0:T(1024)S(1)}, s32[2048]{0:T(1024)}, u32[]{:S(2)}) copy-start(s32[2048]{0:T(1024)} %param.14) | copy-start | bytes 24580
  74.6 15.8 %copy-start.8 = (bf16[128,128]{1,0:T(8,128)(2,1)S(1)}, bf16[128,128]{1,0:T(8,128)(2,1)}, u32[]{:S(2)}) copy-start(bf16[128,128]{1,0:T(8,128)(2,1)} %param.17) | copy-start | bytes 98308
  101.2 7.4 %collective-permute-start.4 = (bf16[1,1024,128]{2,1,0:T(8,128)(2,1)S(1)}, bf16[1,1024,128]{2,1,0:T(8,128)(2,1)S(1)}, u32[]{:S(2)}, u32[]{:S(2)}) collective-permute-start(bf16[1,1024,128]{2,1,0:T(8,128)(2,1)S(1)} %get-tuple-element.31), channel_id=1, source_target_pairs={{0,1},{1,2},{2,3},{3,0},{4,5},{5,6},{6,7},{7,4},{8,9},{9,10},{10,1... | collective-permute-start | bytes 786440 | tf_op jit(solution)/shard_map/ppermute | solution.py:30
  102.5 22.0 %collective-permute-start.5 = (bf16[1,1024,128]{2,1,0:T(8,128)(2,1)S(1)}, bf16[1,1024,128]{2,1,0:T(8,128)(2,1)S(1)}, u32[]{:S(2)}, u32[]{:S(2)}) collective-permute-start(bf16[1,1024,128]{2,1,0:T(8,128)(2,1)S(1)} %get-tuple-element.30), channel_id=1, source_target_pairs={{0,2},{1,3},{2,0},{3,1},{4,6},{5,7},{6,4},{7,5},{8,10},{9,11},{10,... | collective-permute-start | bytes 786440 | tf_op jit(solution)/shard_map/ppermute | solution.py:30
  103.6 23.6 %collective-permute-start.6 = (bf16[1,1024,128]{2,1,0:T(8,128)(2,1)S(1)}, bf16[1,1024,128]{2,1,0:T(8,128)(2,1)S(1)}, u32[]{:S(2)}, u32[]{:S(2)}) collective-permute-start(bf16[1,1024,128]{2,1,0:T(8,128)(2,1)S(1)} %get-tuple-element.29), channel_id=1, source_target_pairs={{0,3},{1,0},{2,1},{3,2},{4,7},{5,4},{6,5},{7,6},{8,11},{9,8},{10,9... | collective-permute-start | bytes 786440 | tf_op jit(solution)/shard_map/ppermute | solution.py:30
